TPU v7x, 128 devices: a whole 4x4x4 slice. The times are simulated.
128 devices in a mesh: sec: 4 (over y_hi, core), dev: 32 (over z, y_lo, x).
Axes of the slice: x: 4, y: 4 (y_hi: 2, y_lo: 2; y = y_hi * 2 + y_lo), z: 4, core: 2. Of those that a mesh axis runs over, the one named last changes fastest.
Arguments:
- queries: bfloat16 [256, 8192], P('dev', 'sec')
- fresh_key_value: bfloat16 [2, 256, 512], P(None, 'dev', 'sec'), may hold values from -6 to 6
- key_value_cache: bfloat16 [2, 256, 1024, 512], P(None, 'dev', None, 'sec'), may hold values from -6 to 6
- lengths: int32 [256], P('dev'), may hold values from 1 to 1024, as said below
- residual: bfloat16 [256, 4096], P(None, 'dev'), may hold values from -6 to 6
- out_weight: bfloat16 [8192, 4096], P('sec', 'dev'), may hold values from -0.0625 to 0.0625
- norm_gain: float32 [4096], P('dev'), may hold values from 0.1 to 1.9
- routes: int32 [256, 8], replicated, may hold values from 0 to 63, all different within a row; in each aligned block of 256 rows (0 to 255, 256 to 511, ...) at most 64 rows name the same one
- route_weights: float32 [256, 8], replicated, may hold values from 0.05 to 0.5
- w_gate: bfloat16 [64, 4096, 1536], P('dev', None, 'sec'), may hold values from -0.09375 to 0.09375
- w_up: bfloat16 [64, 4096, 1536], P('dev', None, 'sec'), may hold values from -0.09375 to 0.09375
- w_down: bfloat16 [64, 1536, 4096], P('dev', 'sec'), may hold values from -0.15625 to 0.15625
Outputs:
- layer_out: bfloat16 [256, 4096], P(None, 'dev')
Inputs may be any that keep to these rules, and one draw needn't show every extreme that they name: `routes`: each row names 8 different experts; no expert is named by more than 64 rows, a bound that some block reaches. `lengths`: some row has all 1024 slots filled.
All inputs are finite; a program needn't handle non-finite values.
Results may differ from a plain program's by a relative error of at most 0.0055.
Values may be sent and summed in bfloat16 or wider, within the bound.
No kernel may reach another device: no remote copies, remote signals or barrier semaphores. Data moves between devices by JAX's collectives and lax.ppermute only.
A program may use at most 128 MiB of HBM per device.

v0:
```python
import math
import jax
import jax.numpy as jnp
from jax import lax
from jax.sharding import PartitionSpec as P

D = 4096
QUERY_HEADS = 64
KEY_VALUE_HEADS = 4
HEAD_SIZE = 128
CAP = 64


def attend(queries, fresh_key_value, key_value_cache, lengths):
    row_count = key_value_cache.shape[1]
    cache_length = key_value_cache.shape[2]
    heads_kv = key_value_cache.shape[3] // HEAD_SIZE
    queries_per_group = QUERY_HEADS // KEY_VALUE_HEADS
    score_scale = 1.0 / math.sqrt(HEAD_SIZE)
    head_queries = queries.reshape(row_count, heads_kv, queries_per_group, HEAD_SIZE)
    cached_keys = key_value_cache[0].reshape(row_count, cache_length, heads_kv, HEAD_SIZE)
    cached_values = key_value_cache[1].reshape(row_count, cache_length, heads_kv, HEAD_SIZE)
    own_key = fresh_key_value[0].reshape(row_count, heads_kv, HEAD_SIZE)
    own_value = fresh_key_value[1].reshape(row_count, heads_kv, HEAD_SIZE).astype(jnp.float32)
    scores = (
        jnp.einsum("rkgd,rtkd->rkgt", head_queries, cached_keys, preferred_element_type=jnp.float32)
        * score_scale
    )
    own_score = (
        jnp.einsum("rkgd,rkd->rkg", head_queries, own_key, preferred_element_type=jnp.float32)
        * score_scale
    )
    visible = (jnp.arange(cache_length, dtype=jnp.int32)[None, :] < lengths[:, None])[
        :, None, None, :
    ]
    row_max = jnp.maximum(jnp.max(jnp.where(visible, scores, -jnp.inf), axis=-1), own_score)
    weights = jnp.where(visible, jnp.exp(scores - row_max[..., None]), 0.0)
    own_weight = jnp.exp(own_score - row_max)
    normalizer = jnp.sum(weights, axis=-1) + own_weight
    weighted = jnp.einsum(
        "rkgt,rtkd->rkgd",
        weights.astype(jnp.bfloat16),
        cached_values,
        preferred_element_type=jnp.float32,
    )
    weighted = weighted + own_weight[..., None] * own_value[:, :, None, :]
    return (
        (weighted / normalizer[..., None])
        .astype(jnp.bfloat16)
        .reshape(row_count, heads_kv * queries_per_group * HEAD_SIZE)
    )


def slot_layout(routes, route_weights, expert_ids):
    matches = routes[:, :, None] == expert_ids[None, None, :]
    chosen = jnp.any(matches, axis=1)
    shares = jnp.sum(jnp.where(matches, route_weights[:, :, None], 0.0), axis=1)
    slot_rank = jnp.cumsum(chosen.astype(jnp.int32), axis=0, dtype=jnp.int32) - 1
    slot_ids = jnp.arange(CAP, dtype=jnp.int32)
    slot_mask = (chosen[:, :, None] & (slot_rank[:, :, None] == slot_ids[None, None, :])).transpose(
        1, 2, 0
    )
    spread = slot_mask.astype(jnp.float32) * shares.T[:, None, :]
    return (slot_mask, spread)


def expert_results(full_rows, slot_mask, w_gate, w_up, w_down):
    picked = jnp.einsum(
        "ecr,rd->ecd", slot_mask.astype(jnp.bfloat16), full_rows, preferred_element_type=jnp.float32
    ).astype(jnp.bfloat16)
    gate_part = jnp.einsum("ecd,edf->ecf", picked, w_gate, preferred_element_type=jnp.float32)
    upward = jnp.einsum("ecd,edf->ecf", picked, w_up, preferred_element_type=jnp.float32)
    activation = (jax.nn.silu(gate_part) * upward).astype(jnp.bfloat16)
    return jnp.einsum("ecf,efd->ecd", activation, w_down, preferred_element_type=jnp.float32)


def shards(
    queries,
    fresh_key_value,
    key_value_cache,
    lengths,
    residual,
    out_weight,
    norm_gain,
    routes,
    route_weights,
    w_gate,
    w_up,
    w_down,
):
    attn = attend(queries, fresh_key_value, key_value_cache, lengths)
    partial_out = jnp.dot(
        lax.all_gather(attn, "dev", axis=0, tiled=True),
        out_weight,
        preferred_element_type=jnp.float32,
    )
    hidden = residual.astype(jnp.float32) + lax.psum(partial_out, "sec")
    square_sum = lax.psum(jnp.sum(hidden * hidden, axis=-1, keepdims=True), "dev")
    normed = (hidden * lax.rsqrt(square_sum / D + 1e-06) * norm_gain).astype(jnp.bfloat16)
    full_rows = lax.all_gather(normed, "dev", axis=1, tiled=True)
    local_count = w_gate.shape[0]
    local_ids = lax.axis_index("dev") * local_count + jnp.arange(local_count, dtype=jnp.int32)
    slot_mask, spread = slot_layout(routes, route_weights, local_ids)
    result = expert_results(full_rows, slot_mask, w_gate, w_up, w_down)
    expert_term = jnp.einsum("ecr,ecd->rd", spread, result, precision=lax.Precision.HIGHEST)
    mixture = lax.psum(lax.psum_scatter(expert_term, "dev", scatter_dimension=1, tiled=True), "sec")
    return (hidden + mixture).astype(jnp.bfloat16)


def solution(mesh):
    return jax.shard_map(
        shards,
        mesh=mesh,
        in_specs=(
            P("dev", "sec"),
            P(None, "dev", "sec"),
            P(None, "dev", None, "sec"),
            P("dev"),
            P(None, "dev"),
            P("sec", "dev"),
            P("dev"),
            P(),
            P(),
            P("dev", None, "sec"),
            P("dev", None, "sec"),
            P("dev", "sec", None),
        ),
        out_specs=P(None, "dev"),
        check_vma=False,
    )
```

profile of v0, /device:TPU:1, one launch (start us, length us, event | category | flops | bytes accessed | tf_op | source)
XLA Modules:
  0.0 653.0 jit_solution(15178874167412993256)
XLA Ops:
  6.5 0.8 bitcast_convert_fusion
  7.3 0.7 iota_compare_fusion.1
  8.0 0.9 fusion.46
  8.9 2.4 select_reduce_fusion
  11.3 0.2 fusion.24
  11.6 2.1 fusion.21
  13.7 0.6 copy.34
  14.3 0.0 all-gather.3.cloned.1.call-update
  14.3 0.0 all-reduce.3.cloned.1.call-start
  14.4 132.9 %all-gather.3.cloned.1.call-done = bf16[256,2048]{1,0:T(8,128)(2,1)} async-done(((bf16[8,2048]{1,0:T(8,128)(2,1)}), bf16[256,2048]{1,0:T(8,128)(2,1)}) %all-gather.3.cloned.1.call-update) | async-done | bytes 1048592 | tf_op jit(solution)/shard_map/all_gather | solution.py:93
  147.2 2.3 fusion.55
  149.5 0.0 all-gather.5.cloned.1.call-start
  149.6 62.2 %all-reduce.3.cloned.1.call-done = f32[256,128]{1,0:T(8,128)} async-done(((f32[256,128]{1,0:T(8,128)}), f32[256,128]{1,0:T(8,128)}) %all-reduce.3.cloned.1.call-update) | async-done | bytes 131088 | tf_op jit(solution)/shard_map/psum | solution.py:97
  211.8 1.0 multiply_reduce_fusion
  212.9 68.0 %psum.22 = f32[256,1]{0,1:T(1,128)S(1)} all-reduce(f32[256,1]{0,1:T(1,128)S(1)} %bitcast.67), channel_id=1, replica_groups=mesh['sec'=4,'dev'=32] {'dev'}, use_global_device_ids=true, to_apply=%region_8.9 | all-reduce | flops 256 | bytes 2048 | tf_op jit(solution)/shard_map/psum | solution.py:98
  280.9 1.6 multiply_convert_fusion
  282.6 0.0 reduce-scatter.2.cloned.1.call-start
  282.6 0.1 compare_reduce_fusion
  282.7 0.6 reduce-window.6
  283.4 0.2 slice_reduce_fusion
  283.6 0.2 reduce-window.9
  283.7 0.1 add_bitcast_fusion
  283.8 0.1 fusion.49
  283.9 116.7 %all-gather.5.cloned.1.call-done = bf16[256,4096]{1,0:T(8,128)(2,1)} async-done(((bf16[256,128]{1,0:T(8,128)(2,1)}), bf16[256,4096]{1,0:T(8,128)(2,1)}) %all-gather.5.cloned.1.call-update) | async-done | bytes 2097168 | tf_op jit(solution)/shard_map/all_gather | solution.py:100
  400.6 2.0 convolution_convert_fusion
  402.6 3.8 fusion.56
  406.4 8.1 %fusion.11 = f32[2,64,4096]{2,1,0:T(8,128)} fusion(bf16[2,384,4096]{2,1,0:T(8,128)(2,1)} %param.23, bf16[2,64,4096]{2,1,0:T(8,128)(2,1)S(1)} %convolution_convert_fusion, bf16[2,4096,384]{2,1,0:T(8,128)(2,1)} %param.22, f32[2,64,384]{2,1,0:T(8,128)S(1)} %fusion.56), kind=kOutput, calls=%fused_computation.12 | convolution fusion | flops 805601280 | bytes 15925248 | tf_op jit(solution)/shard_map/ecf,efd->ecd/dot_general | solution.py:74
  414.5 6.8 %convolution_bitcast_fusion = f32[256,4096]{1,0:T(8,128)} fusion(f32[2,64,4096]{2,1,0:T(8,128)} %fusion.11, f32[2,256]{1,0:T(2,128)S(1)} %bitcast.65, s32[2,256]{1,0:T(2,128)S(1)} %bitcast.58, pred[2,256]{1,0:T(4,128)(4,1)S(1)} %bitcast.62), kind=kOutput, calls=%fused_computation | convolution fusion | flops 1610711040 | bytes 6296064 | tf_op jit(solution)/shard_map/ecr,ecd->rd/dot_general | solution.py:105
  421.3 0.0 all-reduce.5.cloned.1.call-start
  421.4 162.3 %reduce-scatter.2.cloned.1.call-done = f32[256,128]{1,0:T(8,128)} async-done(((f32[256,4096]{1,0:T(8,128)}), f32[256,128]{1,0:T(8,128)}) %reduce-scatter.2.cloned.1.call-update) | async-done | bytes 131088 | tf_op jit(solution)/shard_map/reduce_scatter | solution.py:106
  583.7 61.2 %all-reduce.5.cloned.1.call-done = f32[256,128]{1,0:T(8,128)} async-done(((f32[256,128]{1,0:T(8,128)}), f32[256,128]{1,0:T(8,128)}) %all-reduce.5.cloned.1.call-update) | async-done | bytes 131088 | tf_op jit(solution)/shard_map/psum | solution.py:106
  645.0 1.6 add_convert_fusion
  (24 shorter events, 0.2 us)
Async XLA Ops:
  6.5 140.7 %copy-start = (bf16[2048,128]{1,0:T(8,128)(2,1)S(1)}, bf16[2048,128]{1,0:T(8,128)(2,1)}, u32[]{:S(2)}) copy-start(bf16[2048,128]{1,0:T(8,128)(2,1)} %param.17) | copy-start | bytes 1572868
  6.5 205.3 %copy-start.2 = (bf16[256,128]{1,0:T(8,128)(2,1)S(1)}, bf16[256,128]{1,0:T(8,128)(2,1)}, u32[]{:S(2)}) copy-start(bf16[256,128]{1,0:T(8,128)(2,1)} %param.16) | copy-start | bytes 196612
  6.5 140.7 %all-gather.3.cloned.1.call-start = ((), (), s32[]{:S(2)}) async-start(), calls=%async_computation.1 | async-start | bytes 1081344 | tf_op jit(solution)/shard_map/all_gather | solution.py:93
  8.9 272.0 %copy-start.5 = (f32[128]{0:T(128)S(1)}, f32[128]{0:T(128)}, u32[]{:S(2)}) copy-start(f32[128]{0:T(128)} %param.18) | copy-start | bytes 1540
  8.9 273.7 %copy-start.3 = (s32[256,8]{0,1:T(8,128)S(1)}, s32[256,8]{0,1:T(8,128)}, u32[]{:S(2)}) copy-start(s32[256,8]{0,1:T(8,128)} %param.19) | copy-start | bytes 24580
  8.9 274.9 %copy-start.4 = (f32[256,8]{0,1:T(8,128)S(1)}, f32[256,8]{0,1:T(8,128)}, u32[]{:S(2)}) copy-start(f32[256,8]{0,1:T(8,128)} %param.20) | copy-start | bytes 24580
  14.3 197.5 %all-reduce.3.cloned.1.call-start = ((), (), s32[]{:S(2)}) async-start(), calls=%async_computation.2 | async-start | bytes 262144 | tf_op jit(solution)/shard_map/psum | solution.py:97
  149.5 251.0 %all-gather.5.cloned.1.call-start = ((), (), s32[]{:S(2)}) async-start(), calls=%async_computation.3 | async-start | bytes 2162688 | tf_op jit(solution)/shard_map/all_gather | solution.py:100
  282.6 301.2 %reduce-scatter.2.cloned.1.call-start = ((), (), s32[]{:S(2)}) async-start(), calls=%async_computation.4 | async-start | bytes 4325376 | tf_op jit(solution)/shard_map/reduce_scatter | solution.py:106
  414.5 230.4 %copy-start.1 = (f32[256,128]{1,0:T(8,128)S(1)}, f32[256,128]{1,0:T(8,128)}, u32[]{:S(2)}) copy-start(f32[256,128]{1,0:T(8,128)} %all-reduce.3.cloned.1.call-done) | copy-start | bytes 393220
  421.3 223.6 %all-reduce.5.cloned.1.call-start = ((), (), s32[]{:S(2)}) async-start(), calls=%async_computation.5 | async-start | bytes 262144 | tf_op jit(solution)/shard_map/psum | solution.py:106
Sparse Core Ops, SparseCore 0:
  14.4 132.7 all-gather.2
  149.7 62.0 all-reduce.2
  282.7 117.8 all-gather.4
  421.4 162.2 reduce-scatter.1
  586.2 58.7 all-reduce.4
where the time goes:
time: 654 us; the launch traced here: 653 us
  waiting for transfers between devices  535 us (82%)
  blocking collectives  68 us (10%)
  matrix products  28.3 us (4%)
  between operations  13.2 us (2%)
  other arithmetic  7.04 us (1%)
    reduce_scatter x1, waiting for transfers between devices, shards(): lax.psum_scatter(expert_term, 'dev', scatter_dimension=1, tiled=True)  162 us
    all_gather x1, waiting for transfers between devices, shards(): lax.all_gather(attn, 'dev', axis=0, tiled=True)  133 us
    all_gather x1, waiting for transfers between devices, shards(): full_rows = lax.all_gather(normed, 'dev', axis=1, tiled=True)  117 us
    psum x1, blocking collectives, shards(): lax.psum(jnp.sum(hidden * hidden, axis=-1, keepdims=True), 'dev')  68 us
    psum x1, waiting for transfers between devices, shards(): hidden = residual.astype(jnp.float32) + lax.psum(partial_out, 'sec')  62.2 us
    psum x1, waiting for transfers between devices, shards(): lax.psum(lax.psum_scatter(expert_term, 'dev', scatter_dimension=1, tiled=...  61.2 us
  transfers between devices with their start and end apart: 5, of which 5 were waited for; matrix products, arithmetic and copies ran while one was open for 0% of the time, Pallas kernels for 0%

commit v1 on v0

--- a/solution.py
+++ b/solution.py
@@ -9,6 +9,13 @@
 KEY_VALUE_HEADS = 4
 HEAD_SIZE = 128
 CAP = 64
+
+
+def exchange_gather(x, mesh_axis, dim):
+    size = lax.axis_size(mesh_axis)
+    pieces = jnp.stack([x for _ in range(size)])
+    pieces = lax.all_to_all(pieces, mesh_axis, split_axis=0, concat_axis=0)
+    return jnp.concatenate(pieces, axis=dim)
 
 
 def attend(queries, fresh_key_value, key_value_cache, lengths):
@@ -90,9 +97,7 @@
 ):
     attn = attend(queries, fresh_key_value, key_value_cache, lengths)
     partial_out = jnp.dot(
-        lax.all_gather(attn, "dev", axis=0, tiled=True),
-        out_weight,
-        preferred_element_type=jnp.float32,
+        exchange_gather(attn, "dev", 0), out_weight, preferred_element_type=jnp.float32
     )
     hidden = residual.astype(jnp.float32) + lax.psum(partial_out, "sec")
     square_sum = lax.psum(jnp.sum(hidden * hidden, axis=-1, keepdims=True), "dev")

time: 654 us -> 523 us (0.80)
  waiting for transfers between devices: 535 us -> 381 us
  blocking collectives: 68 us -> 93 us
    all_gather x1 -> x0, waiting for transfers between devices: 133 us -> none  [shards(): lax.all_gather(attn, 'dev', axis=0, tiled=True)]
    all_to_all x0 -> x1, blocking collectives: none -> 24.9 us  [exchange_gather(): pieces = lax.all_to_all(pieces, mesh_axis, split_axis=0, concat_axis=0)]
    psum x1, waiting for transfers between devices: 62.2 us -> 40.9 us  [shards(): hidden = residual.astype(jnp.float32) + lax.psum(partial_out, 'sec')]
  transfers between devices with their start and end apart: 5 -> 4, of which waited for: 5 -> 4; matrix products, arithmetic and copies ran while one was open for 0% -> 0% of each run, Pallas kernels for 0% -> 0%
where the time goes in v1:
time: 523 us; the launch traced here: 522 us
  waiting for transfers between devices  381 us (73%)
  blocking collectives  93 us (18%)
  matrix products  27.1 us (5%)
  between operations  13.2 us (3%)
  other arithmetic  7.03 us (1%)
    reduce_scatter x1, waiting for transfers between devices, shards(): lax.psum_scatter(expert_term, 'dev', scatter_dimension=1, tiled=True)  161 us
    all_gather x1, waiting for transfers between devices, shards(): full_rows = lax.all_gather(normed, 'dev', axis=1, tiled=True)  117 us
    psum x1, blocking collectives, shards(): lax.psum(jnp.sum(hidden * hidden, axis=-1, keepdims=True), 'dev')  68 us
    psum x1, waiting for transfers between devices, shards(): lax.psum(lax.psum_scatter(expert_term, 'dev', scatter_dimension=1, tiled=...  62.3 us
    psum x1, waiting for transfers between devices, shards(): hidden = residual.astype(jnp.float32) + lax.psum(partial_out, 'sec')  40.9 us
    all_to_all x1, blocking collectives, exchange_gather(): pieces = lax.all_to_all(pieces, mesh_axis, split_axis=0, concat_axis=0)  24.9 us
  transfers between devices with their start and end apart: 4, of which 4 were waited for; matrix products, arithmetic and copies ran while one was open for 0% of the time, Pallas kernels for 0%

profile of v1, /device:TPU:1, one launch (start us, length us, event | category | flops | bytes accessed | tf_op | source)
XLA Modules:
  0.0 522.1 jit_solution(13304548301635612657)
XLA Ops:
  6.5 0.8 bitcast_convert_fusion
  7.3 0.7 iota_compare_fusion.1
  8.0 0.9 fusion.48
  8.9 2.4 select_reduce_fusion
  11.3 0.2 fusion.26
  11.6 2.1 fusion.21
  13.7 0.1 stack.3
  13.8 24.9 %all_to_all.5 = bf16[32,8,2048]{2,1,0:T(8,128)(2,1)S(1)} all-to-all(bf16[32,8,2048]{2,1,0:T(8,128)(2,1)S(1)} %stack.3), channel_id=1, replica_groups=mesh['sec'=4,'dev'=32] {'dev'}, dimensions={0} | all-to-all | bytes 2097152 | tf_op jit(solution)/shard_map/all_to_all | solution.py:17
  38.8 1.1 fusion.24
  39.8 0.0 all-reduce.3.cloned.1.call-update
  39.9 0.0 all-gather.2.cloned.1.call-start
  39.9 40.9 %all-reduce.3.cloned.1.call-done = f32[256,128]{1,0:T(8,128)} async-done(((f32[256,128]{1,0:T(8,128)}), f32[256,128]{1,0:T(8,128)}) %all-reduce.3.cloned.1.call-update) | async-done | bytes 131088 | tf_op jit(solution)/shard_map/psum | solution.py:102
  80.8 1.0 multiply_reduce_fusion
  81.8 68.0 %psum.22 = f32[256,1]{0,1:T(1,128)S(1)} all-reduce(f32[256,1]{0,1:T(1,128)S(1)} %bitcast.69), channel_id=1, replica_groups=mesh['sec'=4,'dev'=32] {'dev'}, use_global_device_ids=true, to_apply=%region_8.9 | all-reduce | flops 256 | bytes 2048 | tf_op jit(solution)/shard_map/psum | solution.py:103
  149.8 1.6 multiply_convert_fusion
  151.5 0.0 reduce-scatter.2.cloned.1.call-start
  151.6 0.1 compare_reduce_fusion
  151.7 0.6 reduce-window.6
  152.3 0.2 slice_reduce_fusion
  152.5 0.2 reduce-window.9
  152.7 0.1 add_bitcast_fusion
  152.8 0.1 fusion.51
  152.9 116.7 %all-gather.2.cloned.1.call-done = bf16[256,4096]{1,0:T(8,128)(2,1)} async-done(((bf16[256,128]{1,0:T(8,128)(2,1)}), bf16[256,4096]{1,0:T(8,128)(2,1)}) %all-gather.2.cloned.1.call-update) | async-done | bytes 2097168 | tf_op jit(solution)/shard_map/all_gather | solution.py:105
  269.5 2.0 convolution_convert_fusion
  271.6 3.8 fusion.57
  275.4 8.1 %fusion.11 = f32[2,64,4096]{2,1,0:T(8,128)} fusion(bf16[2,384,4096]{2,1,0:T(8,128)(2,1)} %param.23, bf16[2,64,4096]{2,1,0:T(8,128)(2,1)S(1)} %convolution_convert_fusion, bf16[2,4096,384]{2,1,0:T(8,128)(2,1)} %param.22, f32[2,64,384]{2,1,0:T(8,128)S(1)} %fusion.57), kind=kOutput, calls=%fused_computation.12 | convolution fusion | flops 805601280 | bytes 15925248 | tf_op jit(solution)/shard_map/ecf,efd->ecd/dot_general | solution.py:81
  283.5 6.8 %convolution_bitcast_fusion = f32[256,4096]{1,0:T(8,128)} fusion(f32[2,64,4096]{2,1,0:T(8,128)} %fusion.11, f32[2,256]{1,0:T(2,128)S(1)} %bitcast.67, s32[2,256]{1,0:T(2,128)S(1)} %bitcast.60, pred[2,256]{1,0:T(4,128)(4,1)S(1)} %bitcast.64), kind=kOutput, calls=%fused_computation | convolution fusion | flops 1610711040 | bytes 6296064 | tf_op jit(solution)/shard_map/ecr,ecd->rd/dot_general | solution.py:110
  290.2 0.0 reduce-scatter.2.cloned.1.call-update
  290.3 0.0 all-reduce.5.cloned.1.call-start
  290.3 161.3 %reduce-scatter.2.cloned.1.call-done = f32[256,128]{1,0:T(8,128)} async-done(((f32[256,4096]{1,0:T(8,128)}), f32[256,128]{1,0:T(8,128)}) %reduce-scatter.2.cloned.1.call-update) | async-done | bytes 131088 | tf_op jit(solution)/shard_map/reduce_scatter | solution.py:111
  451.7 62.3 %all-reduce.5.cloned.1.call-done = f32[256,128]{1,0:T(8,128)} async-done(((f32[256,128]{1,0:T(8,128)}), f32[256,128]{1,0:T(8,128)}) %all-reduce.5.cloned.1.call-update) | async-done | bytes 131088 | tf_op jit(solution)/shard_map/psum | solution.py:111
  514.0 1.6 add_convert_fusion
  (23 shorter events, 0.1 us)
Async XLA Ops:
  6.5 32.2 %copy-start = (bf16[2048,128]{1,0:T(8,128)(2,1)S(1)}, bf16[2048,128]{1,0:T(8,128)(2,1)}, u32[]{:S(2)}) copy-start(bf16[2048,128]{1,0:T(8,128)(2,1)} %param.17) | copy-start | bytes 1572868
  6.5 74.2 %all-reduce.3.cloned.1.call-start = ((), (), s32[]{:S(2)}) async-start(), calls=%async_computation.2 | async-start | bytes 262144 | tf_op jit(solution)/shard_map/psum | solution.py:102
  11.5 69.3 %copy-start.2 = (bf16[256,128]{1,0:T(8,128)(2,1)S(1)}, bf16[256,128]{1,0:T(8,128)(2,1)}, u32[]{:S(2)}) copy-start(bf16[256,128]{1,0:T(8,128)(2,1)} %param.16) | copy-start | bytes 196612
  11.5 138.3 %copy-start.5 = (f32[128]{0:T(128)S(1)}, f32[128]{0:T(128)}, u32[]{:S(2)}) copy-start(f32[128]{0:T(128)} %param.18) | copy-start | bytes 1540
  11.6 140.0 %copy-start.3 = (s32[256,8]{0,1:T(8,128)S(1)}, s32[256,8]{0,1:T(8,128)}, u32[]{:S(2)}) copy-start(s32[256,8]{0,1:T(8,128)} %param.19) | copy-start | bytes 24580
  11.6 141.2 %copy-start.4 = (f32[256,8]{0,1:T(8,128)S(1)}, f32[256,8]{0,1:T(8,128)}, u32[]{:S(2)}) copy-start(f32[256,8]{0,1:T(8,128)} %param.20) | copy-start | bytes 24580
  39.9 229.7 %all-gather.2.cloned.1.call-start = ((), (), s32[]{:S(2)}) async-start(), calls=%async_computation.3 | async-start | bytes 2162688 | tf_op jit(solution)/shard_map/all_gather | solution.py:105
  151.5 300.1 %reduce-scatter.2.cloned.1.call-start = ((), (), s32[]{:S(2)}) async-start(), calls=%async_computation.4 | async-start | bytes 4325376 | tf_op jit(solution)/shard_map/reduce_scatter | solution.py:111
  283.5 230.5 %copy-start.1 = (f32[256,128]{1,0:T(8,128)S(1)}, f32[256,128]{1,0:T(8,128)}, u32[]{:S(2)}) copy-start(f32[256,128]{1,0:T(8,128)} %all-reduce.3.cloned.1.call-done) | copy-start | bytes 393220
  290.3 223.7 %all-reduce.5.cloned.1.call-start = ((), (), s32[]{:S(2)}) async-start(), calls=%async_computation.5 | async-start | bytes 262144 | tf_op jit(solution)/shard_map/psum | solution.py:111
Sparse Core Ops, SparseCore 0:
  40.0 40.7 all-reduce.2
  151.6 117.8 all-gather.1
  290.4 161.2 reduce-scatter.1
  454.1 59.8 all-reduce.4
